TPU v7x, 32 devices: a whole 2x2x4 slice. The times are simulated.
32 devices in a mesh: rep: 2 (over x), fsdp: 4 (over y, core), seq: 4 (over z).
Axes of the slice: x: 2, y: 2, z: 4, core: 2. Of those that a mesh axis runs over, the one named last changes fastest.
Arguments:
- tokens: bfloat16 [2, 16, 1024, 768], P(None, ('rep', 'fsdp'), 'seq'), may hold values from -6 to 6
- segments: int32 [2, 16, 1024], P(None, ('rep', 'fsdp')), may hold values from 0 to 1023, as said below
- positions: int32 [2, 16, 1024], P(None, ('rep', 'fsdp'), 'seq'), may hold values from 0 to 1023, as said below
- gain_attn: bfloat16 [768], P('fsdp'), may hold values from 0.5 to 1.5
- w_qkv: bfloat16 [768, 2304], P('fsdp'), may hold values from -0.21875 to 0.21875
- w_out: bfloat16 [768, 768], P('fsdp'), may hold values from -0.875 to 0.875
- gain_mlp: bfloat16 [768], P('fsdp'), may hold values from 0.5 to 1.5
- w_in: bfloat16 [768, 2304], P('fsdp'), may hold values from -0.21875 to 0.21875
- w_mlp_out: bfloat16 [1152, 768], P('fsdp'), may hold values from -0.375 to 0.375
- cotangent: bfloat16 [2, 16, 1024, 768], P(None, ('rep', 'fsdp'), 'seq'), may hold values from -6 to 6
Outputs:
- block_out: bfloat16 [2, 16, 1024, 768], P(None, ('rep', 'fsdp'), 'seq')
- input_grad: float32 [2, 16, 1024, 768], P(None, ('rep', 'fsdp'), 'seq')
- grad_gain_attn: float32 [768], P('fsdp')
- grad_qkv: float32 [768, 2304], P('fsdp')
- grad_out: float32 [768, 768], P('fsdp')
- grad_gain_mlp: float32 [768], P('fsdp')
- grad_in: float32 [768, 2304], P('fsdp')
- grad_mlp_out: float32 [1152, 768], P('fsdp')
Inputs may be any that keep to these rules, and one draw needn't show every extreme that they name: `segments`: along each sequence segment numbers start at 0, never fall and rise by one where a new document begins; documents range from a single token to the whole sequence. `positions`: each token's position is 0 at the first token of its document (as given by segments) and rises by one along the document.
All inputs are finite; a program needn't handle non-finite values.
Results may differ from a plain program's by a relative error of at most 0.02.
Values may be sent and summed in bfloat16 or wider, within the bound.
A program may use at most 192 MiB of HBM per device.

v0:
```python
import functools
import math

import jax
import jax.numpy as jnp
from jax import lax
from jax.experimental import pallas as pl
from jax.experimental.pallas import tpu as pltpu
from jax.sharding import PartitionSpec as P

D = 768
HEADS = 12
HDIM = 64
FF = 1152
EPS = 1e-05
THETA = 160000.0
MASKED = -1000000000.0
QUERY_SCALE = HDIM**-0.5 / math.log(2.0)
TILE = 256
PAIR = 2 * HDIM
WIDE = 384
HCHUNK = 384
f32 = jnp.float32
bf16 = jnp.bfloat16
VMEM_LIMIT = 62 * 2**20


def dot_nn(left, right):
    return lax.dot_general(left, right, (((1,), (0,)), ((), ())), preferred_element_type=f32)


def dot_nt(left, right):
    return lax.dot_general(left, right, (((1,), (1,)), ((), ())), preferred_element_type=f32)


def dot_tn(left, right):
    return lax.dot_general(left, right, (((0,), (0,)), ((), ())), preferred_element_type=f32)


def normalize(values):
    mean = jnp.mean(values, axis=-1, keepdims=True)
    centered = values - mean
    var = jnp.mean(centered * centered, axis=-1, keepdims=True)
    scale = lax.rsqrt(var + EPS)
    return centered * scale, scale


def norm_back(unit, scale, gain, grad):
    gain_terms = grad * unit
    inner = grad * gain
    first = jnp.mean(inner, axis=-1, keepdims=True)
    second = jnp.mean(inner * unit, axis=-1, keepdims=True)
    return scale * (inner - first - unit * second), gain_terms


def lane_halves(shape):
    lane = lax.broadcasted_iota(jnp.int32, shape, len(shape) - 1)
    return lane % HDIM < HDIM // 2


def rotate_pair(values, cosine, signed_sine):
    swapped = jnp.where(
        lane_halves(values.shape),
        pltpu.roll(values, PAIR - HDIM // 2, 1),
        pltpu.roll(values, HDIM // 2, 1),
    )
    return values * cosine + swapped * signed_sine


def first_kernel(x_ref, gain_ref, w_ref, cos_ref, sin_ref, a_ref, qkv_ref):
    unit, _ = normalize(x_ref[...].astype(f32))
    a = (unit * gain_ref[0:1, :]).astype(bf16)
    a_ref[...] = a
    cosine, sine = cos_ref[...], sin_ref[...]
    for column in range(0, 3 * D, TILE):
        part = dot_nn(a, w_ref[:, column : column + TILE])
        for half in range(0, TILE, PAIR):
            start = column + half
            piece = part[:, half : half + PAIR]
            if start < 2 * D:
                piece = rotate_pair(piece, cosine, sine)
            if start < D:
                piece = piece * QUERY_SCALE
            qkv_ref[:, start : start + PAIR] = piece.astype(bf16)


def head_lanes():
    lane = lax.broadcasted_iota(jnp.int32, (1, PAIR), 1)
    return [lane < HDIM, lane >= HDIM]


def attend_pair(q_ref, k_ref, v_ref, rows_ref, cols_ref, p_ref, inv_ref, write):
    k, v = k_ref[...], v_ref[...]
    length = k.shape[0]
    mine = head_lanes()
    zero, one = jnp.zeros((), bf16), jnp.ones((), bf16)
    summing = [jnp.where(m, v, one) for m in mine]
    items = [(tile, head) for tile in range(0, length, TILE) for head in range(2)]

    def score(item):
        tile, head = item
        return dot_nt(jnp.where(mine[head], q_ref[tile : tile + TILE, :], zero), k)

    ahead = score(items[0])
    kept = None
    for i, (tile, head) in enumerate(items):
        rows = slice(tile, tile + TILE)
        scores = ahead
        if i + 1 < len(items):
            ahead = score(items[i + 1])
        scores = jnp.where(rows_ref[rows, :] == cols_ref[...], scores, MASKED)
        probs = jnp.exp2(scores - jnp.max(scores, axis=-1, keepdims=True)).astype(bf16)
        p_ref[head, rows, :] = probs
        part = dot_nn(probs, summing[head])
        inv = 1.0 / pltpu.roll(part, HDIM, 1)
        if head == 0:
            kept = (part * inv, inv)
        else:
            inv_ref[rows, :] = jnp.where(mine[0], kept[1], inv)
            write(rows, jnp.where(mine[0], kept[0], part * inv).astype(bf16))


def forward_kernel(
    sizes, pairs, late, q_ref, k_ref, v_ref, rows_ref, cols_ref, x_ref, gain_ref, w_out_any, w_in_any, w_mlp_any, cot_ref,
    o_ref, p_ref, inv_ref, x1_ref, b_ref, m_ref, slope_ref, act_ref, y_ref, dy_ref, *refs,
):
    seq = sizes[2]
    refs = list(refs)
    outs = [refs.pop(0) for _ in range(2 * late)]
    joined, w_out_ref, w_in_ref, w_mlp_ref, bounce, *sem_refs = refs
    step, last = pl.program_id(0), pl.num_programs(0) - 1
    sems = Sems(*sem_refs)
    me_seq = lax.axis_index("seq")
    into = sems.copy(cot_ref.at[me_seq], bounce)
    outof = sems.copy(bounce, dy_ref.at[0])
    weights = [sems.copy(w_out_any, w_out_ref)]
    partners = [("seq", k) for k in range(1, seq)]
    if late:
        gather = LateGather(sizes, [w_in_any, w_mlp_any], [w_in_ref, w_mlp_ref], sems)
        weights += gather.own
        keeps = [sems.copy(w_in_ref, outs[0]), sems.copy(w_mlp_ref, outs[1])]
        partners = all_partners(sizes)
    else:
        weights += [sems.copy(w_in_any, w_in_ref), sems.copy(w_mlp_any, w_mlp_ref)]
    blocks = [sems.remote(cot_ref.at[flip(me_seq, k)], dy_ref.at[k], "seq", k) for k in range(1, seq)]

    @pl.when(step == 0)
    def _():
        into.start()
        start_all(weights)
        meet(partners)
        if late:
            start_all(gather.far)
        start_all(blocks)
        into.wait()
        outof.start()

    if late:
        for when in range(1, pairs + 1):
            @pl.when(step == when)
            def _(when=when):
                gather.advance(when)

    @pl.when(step < pairs)
    def _():
        def write(rows, value):
            o_ref[rows, :] = value
            joined[rows, pl.ds(pl.multiple_of(step * PAIR, PAIR), PAIR)] = value

        attend_pair(q_ref, k_ref, v_ref, rows_ref, cols_ref, p_ref, inv_ref, write)

    @pl.when(step == pairs)
    def _():
        if late:
            wait_all(weights[:1])
            gather.finish(0)
            keeps[0].start()
        else:
            wait_all(weights)

    @pl.when(step >= pairs)
    def _():
        start = pl.multiple_of((step - pairs) * TILE, TILE)
        x1 = x_ref[...].astype(f32) + dot_nn(joined[pl.ds(start, TILE), :], w_out_ref[...])
        x1_ref[...] = x1
        unit, _ = normalize(x1)
        b = (unit * gain_ref[1:2, :]).astype(bf16)
        b_ref[...] = b

        def hidden(column):
            return (
                dot_nn(b, w_in_ref[:, column : column + HCHUNK]),
                dot_nn(b, w_in_ref[:, FF + column : FF + column + HCHUNK]),
            )

        ahead = hidden(0)
        for column in range(0, FF, HCHUNK):
            hin, gate = ahead
            if column + HCHUNK < FF:
                ahead = hidden(column + HCHUNK)
            phi = 0.5 + 0.5 * lax.erf(hin * math.sqrt(0.5))
            act = hin * phi
            slope = phi + hin * (jnp.exp(hin * hin * -0.5) * (1.0 / math.sqrt(2.0 * math.pi)))
            m_ref[:, column : column + HCHUNK] = (act * gate).astype(bf16)
            act_ref[:, column : column + HCHUNK] = act.astype(bf16)
            slope_ref[:, column : column + HCHUNK] = (slope * gate).astype(bf16)
        if late:
            @pl.when(step == pairs)
            def _():
                gather.finish(1)
                keeps[1].start()

        y_ref[...] = (x1_ref[...] + dot_nn(m_ref[...], w_mlp_ref[...])).astype(bf16)

    @pl.when(step == last)
    def _():
        if late:
            wait_all(keeps)
        outof.wait()
        wait_all(blocks)


def order_of(sizes, rep_first):
    fsdp, rep, seq = sizes
    core = [("fsdp", 1)]
    rest = [("fsdp", b) for b in bits_of(fsdp)[1:]]
    copies = [("rep", b) for b in bits_of(rep)]
    return core + (copies + rest if rep_first else rest + copies) + [("seq", b) for b in bits_of(seq)]


def all_partners(sizes):
    fsdp, rep, seq = sizes
    return [("seq", k) for k in range(1, seq)] + [("fsdp", b) for b in bits_of(fsdp)] + [("rep", b) for b in bits_of(rep)]


def early_reducers(sizes):
    fsdp, rep, seq = sizes
    shapes = [(fsdp, FF // fsdp, D), (fsdp, D // fsdp, FF), (fsdp, D // fsdp, FF), (fsdp, D // fsdp, D)]
    reducers = [Reducer(shape, sizes, order_of(sizes, w == 2)) for w, shape in enumerate(shapes)]
    across = len(bits_of(fsdp)) + len(bits_of(rep))
    return reducers, [len(reducers[0].steps)] + [across + 2] * 2 + [across + 1]


def late_reducers(sizes):
    fsdp = sizes[0]
    return [Reducer((fsdp, D // fsdp, D), sizes, order_of(sizes, w == 1)) for w in range(3)]


def flat(rows):
    return rows % 16 == 0


def shard_of(ref, rows, q):
    return ref.at[pl.ds(pl.multiple_of(q * rows, 16), rows)] if flat(rows) else ref.at[q]


def weight_gradient(ref, wide, left, right):
    if len(ref.shape) == 2:
        @pl.loop(0, ref.shape[0] // HCHUNK)
        def _(i):
            at = pl.ds(pl.multiple_of(i * HCHUNK, HCHUNK), HCHUNK)
            ref[at, :] = dot_tn(left[:, at], right[...]).astype(bf16)
    else:
        shards, rows, cols = ref.shape
        wide[: shards * rows, :cols] = dot_tn(left[...], right[...])
        for q in range(shards):
            ref[q] = wide[q * rows : (q + 1) * rows, :cols].astype(bf16)


def middle_back_tile(dy, x1_ref, slope_ref, act_ref, gain_ref, w_out_ref, w_in_ref, w_mlp_ref, dh_ref, dgain_ref, dx1_ref):
    ahead = dot_nt(dy, w_mlp_ref[:HCHUNK, :])
    for column in range(0, FF, HCHUNK):
        dm = ahead
        if column + HCHUNK < FF:
            ahead = dot_nt(dy, w_mlp_ref[column + HCHUNK : column + 2 * HCHUNK, :])
        dh_ref[:, column : column + HCHUNK] = (dm * slope_ref[:, column : column + HCHUNK].astype(f32)).astype(bf16)
        dh_ref[:, FF + column : FF + column + HCHUNK] = (
            dm * act_ref[:, column : column + HCHUNK].astype(f32)
        ).astype(bf16)
    db = dot_nt(dh_ref[...], w_in_ref[...])
    unit, scale = normalize(x1_ref[...])
    back, terms = norm_back(unit, scale, gain_ref[1:2, :], db)
    dgain_ref[...] += jnp.sum(terms, axis=0, keepdims=True)
    dx1 = dy.astype(f32) + back
    dx1_ref[...] = dx1
    return dx1.astype(bf16)


def attend_back_pair(q_ref, k_ref, v_ref, o_ref, inv_ref, do, p_ref, cos_ref, sin_ref, dq_ref, dk_ref, dv_ref):
    v = v_ref[...]
    length = v.shape[0]
    mine = head_lanes()
    zero = jnp.zeros((), bf16)
    do = (do.astype(f32) * inv_ref[...]).astype(bf16)
    inner = do.astype(f32) * o_ref[...].astype(f32)
    do_heads = [jnp.where(m, do, zero) for m in mine]
    q_heads = [jnp.where(m, q_ref[...], zero).T for m in mine]
    k_heads = [jnp.where(m, k_ref[...], zero) for m in mine]
    do_turned = [d.T for d in do_heads]
    cosine, sine = cos_ref[...], sin_ref[...]
    dv = dk = None
    for tile in range(0, length, TILE):
        rows = slice(tile, tile + TILE)
        dq = None
        for head in range(2):
            probs = p_ref[head, rows, :]
            delta = jnp.sum(jnp.where(mine[head], inner[rows], 0.0), axis=-1, keepdims=True)
            dp = dot_nt(do_heads[head][rows], v)
            ds = (probs.astype(f32) * (dp - delta)).astype(bf16)
            value_part = dot_nn(do_turned[head][:, rows], probs)
            key_part = dot_nn(q_heads[head][:, rows], ds)
            query_part = dot_nn(ds, k_heads[head])
            dv = value_part if dv is None else dv + value_part
            dk = key_part if dk is None else dk + key_part
            dq = query_part if dq is None else dq + query_part
        dq_ref[rows, :] = rotate_pair(dq * HDIM**-0.5, cosine[rows], -sine[rows]).astype(bf16)
    dk_ref[...] = rotate_pair(dk.T * math.log(2.0), cosine, -sine).astype(bf16)
    dv_ref[...] = dv.T.astype(bf16)


def backward_kernel(
    sizes, tiles, x1_ref, slope_ref, act_ref, gain_ref, q_ref, k_ref, v_ref, o_ref, inv_ref,
    p_any, cos_any, sin_any, w_out_any, w_in_any, w_mlp_any, m_any, dy_any, b_any, o_any, y_ref, *refs,
):
    reducers, early = early_reducers(sizes)
    count = len(reducers)
    refs = list(refs)
    pop = lambda n: [refs.pop(0) for _ in range(n)]
    dx1_ref, dgain_ref, dq_ref, dk_ref, dv_ref, home_ref = pop(6)
    sums_out = pop(count)
    w_out_ref, w_in_ref, w_mlp_ref, m_ref, dy_ref, b_ref, all_o_ref = pop(7)
    dh_ref, low_ref, do_ref, wide, bounce, probs_ref, cos_ref, sin_ref = pop(8)
    grads = pop(count)
    (mlp_final,) = pop(1)
    lands = [pop(len(r.scratch(0, e))) for r, e in zip(reducers, early)]
    sems = Sems(*refs)
    me = lax.axis_index("fsdp")
    step, last = pl.program_id(0), pl.num_programs(0) - 1
    into, outof, blocks = give_back(y_ref, home_ref, bounce, sems)
    loads = [
        sems.copy(src, dst)
        for src, dst in [
            (m_any, m_ref), (dy_any, dy_ref), (w_mlp_any, w_mlp_ref), (w_in_any, w_in_ref), (w_out_any, w_out_ref),
            (b_any, b_ref), (o_any, all_o_ref), (cos_any, cos_ref), (sin_any, sin_ref),
        ]
    ]
    pair, pairs = step - tiles - 1, last - tiles
    slot_sems = [sems.local.at[sems.local_used + i] for i in range(2)]
    sems.local_used += 2

    def fetch(which, slot):
        return pltpu.make_async_copy(p_any.at[pl.ds(which * 2, 2)], probs_ref.at[slot], slot_sems[slot])
    stores = [sems.copy(mlp_final if w == 0 else shard_of(grads[w], reducers[w].rows, me), sums_out[w]) for w in range(count)]
    for w, reducer in enumerate(reducers):
        reducer.bind(lambda j, w=w: shard_of(grads[w], reducers[w].rows, flip(me, j)), lands[w], sems, 0, early[w], mlp_final if w == 0 else None)
    mlp, first_half, second_half, out = reducers

    def at(when, *actions):
        @pl.when(step == when)
        def _():
            for action in actions:
                action()

    def advance(reducer, s, limit):
        def run():
            reducer.finish(s)
            if s + 1 < limit:
                reducer.start(s + 1)
        return run

    @pl.when(step == 0)
    def _():
        start_all(loads)
        into.start()
        meet(all_partners(sizes))
        start_all(blocks)
        dgain_ref[...] = jnp.zeros_like(dgain_ref)
        wait_all(loads[:2])
        weight_gradient(grads[0], wide, m_ref, dy_ref)
        mlp.start(0)
        into.wait()
        outof.start()
        wait_all(loads[2:5])

    at(1, advance(mlp, 0, early[0]))

    @pl.when(step < tiles)
    def _():
        rows = pl.ds(pl.multiple_of(step * TILE, TILE), TILE)
        low = middle_back_tile(
            dy_ref[rows, :], x1_ref, slope_ref, act_ref, gain_ref, w_out_ref, w_in_ref, w_mlp_ref,
            dh_ref.at[rows, :], dgain_ref, dx1_ref,
        )
        low_ref[rows, :] = low
        do_ref[rows, :] = dot_nt(low, w_out_ref[...]).astype(bf16)

    across = len(bits_of(sizes[0])) + len(bits_of(sizes[1]))

    @pl.when(step == tiles)
    def _():
        wait_all(loads[5:])
        weight_gradient(grads[1], wide, b_ref, dh_ref.at[:, :FF])
        first_half.start(0)
        weight_gradient(grads[2], wide, b_ref, dh_ref.at[:, FF:])
        second_half.start(0)
        for s in range(1, across - 1):
            advance(mlp, s, early[0])()
        weight_gradient(grads[3], wide, all_o_ref, low_ref)
        out.start(0)

    @pl.when(step == tiles - 1)
    def _():
        fetch(0, 0).start()

    for slot in range(2):
        @pl.when((step > tiles) & (pair % 2 == slot))
        def _(slot=slot):
            fetch(pair, slot).wait()

            @pl.when(pair + 1 < pairs)
            def _():
                fetch(pair + 1, 1 - slot).start()

    halves = (first_half, second_half)
    steps = lambda reducer, limit, *which: [advance(reducer, s, limit) for s in which]
    half_steps = lambda *which: [advance(r, s, early[1]) for s in which for r in halves]
    middle = range(1, across - 1)
    at(tiles + 1, *steps(mlp, early[0], across - 1), *half_steps(0))
    at(tiles + 2, *steps(out, early[3], 0))
    at(tiles + 3, *half_steps(*middle))
    at(tiles + 4, *steps(mlp, early[0], across), *steps(out, early[3], *middle))
    at(tiles + 5, *steps(mlp, early[0], across + 1), *half_steps(across - 1))
    at(tiles + 6, *steps(mlp, early[0], *range(across + 2, early[0] - 1)), *half_steps(across), *steps(out, early[3], across - 1))

    @pl.when(step > tiles)
    def _():
        column = pl.multiple_of(pair * PAIR, PAIR)
        attend_back_pair(
            q_ref, k_ref, v_ref, o_ref, inv_ref, do_ref[:, pl.ds(column, PAIR)], probs_ref.at[pair % 2], cos_ref, sin_ref,
            dq_ref, dk_ref, dv_ref,
        )

    @pl.when(step == last)
    def _():
        for w, reducer in enumerate(reducers):
            reducer.finish(early[w] - 1)
            stores[w].start()
        wait_all(stores)
        outof.wait()
        wait_all(blocks)


PIECES = 4


def leave_kernel(sizes, gain_ref, other_gain_ref, *refs):
    fsdp, rep, seq = sizes
    reducers, early = (some[1:] for some in early_reducers(sizes))
    whole = late_reducers(sizes)
    count, more = len(reducers), len(whole)
    refs = list(refs)
    pop = lambda n: [refs.pop(0) for _ in range(n)]
    anys = pop(7)
    sums_in = pop(count)
    (home_ref,) = pop(1)
    in_out, out_out, qkv_out, gains_out = pop(4)
    dq_ref, a_ref, dk_ref, dv_ref, w_ref, x_ref, dx1_ref = local = pop(7)
    slots, wide, in_final, out_final, qkv_final = pop(5)
    held, grads = pop(count), pop(more)
    lands = [pop(len(r.scratch(e, len(r.steps)))) for r, e in zip(reducers, early)]
    whole_lands = [pop(len(r.scratch(0, len(r.steps)))) for r in whole]
    (gain_lands,) = pop(1)
    sems = Sems(*refs)
    me, me_seq = lax.axis_index("fsdp"), lax.axis_index("seq")
    own = sems.copy(slots.at[0], home_ref.at[me_seq])
    height = slots.shape[1] // PIECES
    blocks = {
        k: [
            sems.remote(slots.at[k, pl.ds(n * height, height)], home_ref.at[me_seq, pl.ds(n * height, height)], "seq", k)
            for n in range(PIECES)
        ]
        for k in range(1, seq)
    }
    order = sorted(range(1, seq), key=lambda k: (k != 2, k == 1))
    ready = []

    def send_piece(n=1):
        for _ in range(n):
            if ready:
                ready.pop(0).start()

    operands = [sems.copy(src, dst) for src, dst in zip(anys, local)]
    loads = [sems.copy(sums_in[w], held[w]) for w in range(count)]
    stores = [
        sems.copy(src, dst)
        for src, dst in ((in_final, in_out), (out_final, out_out), (qkv_final, qkv_out))
    ]
    finals = [in_final.at[:, pl.ds(0, FF)], in_final.at[:, pl.ds(FF, FF)], out_final]
    for w, reducer in enumerate(reducers):
        reducer.bind(lambda j, w=w: held[w], lands[w], sems, early[w], len(reducer.steps), finals[w])
    for w, reducer in enumerate(whole):
        reducer.bind(
            lambda j, w=w: shard_of(grads[w], whole[w].rows, flip(me, j)), whole_lands[w], sems, 0, len(reducer.steps),
            qkv_final.at[:, pl.ds(w * D, D)],
        )
    hops = [("fsdp", b) for b in bits_of(fsdp)] + [("rep", b) for b in bits_of(rep)] + [("seq", b) for b in bits_of(seq)]
    gain_moves = [sems.remote(gains_out, gain_lands.at[i], axis, bit) for i, (axis, bit) in enumerate(hops)]
    rows = slots.shape[1]

    def advance(some, s):
        for reducer in some:
            if s < len(reducer.steps):
                reducer.finish(s)
                if s + 1 < len(reducer.steps):
                    reducer.start(s + 1)

    def advance_gains(i):
        if i < len(hops):
            gain_moves[i].wait()
            gains_out[...] += gain_lands[i]
            if i + 1 < len(hops):
                gain_moves[i + 1].start()

    def input_slot(k):
        piece = slice(k * rows, (k + 1) * rows)
        da = dot_nt(dq_ref[piece, :], w_ref[:, :D])
        da = da + dot_nt(dk_ref[piece, :], w_ref[:, D : 2 * D])
        da = da + dot_nt(dv_ref[piece, :], w_ref[:, 2 * D :])
        unit, scale = normalize(x_ref[piece, :].astype(f32))
        back, terms = norm_back(unit, scale, gain_ref[0:1, :], da)
        gains_out[0:1, :] += jnp.sum(terms, axis=0, keepdims=True)
        slots[k] = (dx1_ref[piece, :] + back).astype(bf16)
        if k:
            ready.extend(blocks[k])

    def gradient(w, part):
        weight_gradient(grads[w], wide, a_ref, part)
        whole[w].start(0)

    across = len(bits_of(fsdp)) + len(bits_of(rep))
    halves, out, last = reducers[:2], reducers[2:], len(whole[0].steps)
    start_all(operands[:2])
    start_all(loads)
    start_all(operands[2:])
    gains_out[...] = jnp.zeros_like(gains_out)
    gains_out[1:2, :] = other_gain_ref[...]
    meet(all_partners(sizes))
    wait_all(loads)
    for w, (reducer, s) in enumerate(zip(reducers, early)):
        if s < len(reducer.steps):
            reducer.start(s)
        else:
            finals[w][...] = held[w][...]
    wait_all(operands[:2])
    gradient(0, dq_ref)
    wait_all(operands[2:])
    input_slot(order[0])
    send_piece(PIECES // 2)
    advance(whole[:1], 0)
    advance(halves, early[0])
    gradient(1, dk_ref)
    for k in order[1:2]:
        input_slot(k)
    advance(whole[1:2], 0)
    advance(out, early[2])
    send_piece()
    gradient(2, dv_ref)
    for k in order[2:]:
        input_slot(k)
    advance(whole[:1], 1)
    advance(whole[2:], 0)
    send_piece()
    input_slot(0)
    own.start()
    gain_moves[0].start()
    advance(whole[1:2], 1)
    advance(out, early[2] + 1)
    send_piece()
    for s in range(2, across):
        advance(whole[:1], s)
        advance(whole[2:], s - 1)
        advance(whole[1:2], s)
        send_piece()
    advance(whole[2:], across - 1)
    send_piece()
    i = 0
    for s in range(across, last):
        for reducer in whole:
            advance([reducer], s)
            send_piece()
        for _ in range(2):
            advance_gains(i)
            i += 1
    while i < len(hops):
        advance_gains(i)
        i += 1
    send_piece(len(ready))
    for s in range(early[0] + 1, len(halves[0].steps)):
        advance(halves, s)
    for s in range(early[2] + 2, len(out[0].steps)):
        advance(out, s)
    start_all(stores)
    wait_all(stores)
    own.wait()
    for k in range(1, seq):
        wait_all(blocks[k])


def rows_spec(width):
    return pl.BlockSpec((TILE, width), lambda i: (i, 0))


def whole_spec(*shape):
    return pl.BlockSpec(shape, lambda i: (0,) * len(shape))


def pair_spec(length, offset=0):
    return pl.BlockSpec((length, PAIR), lambda i: (0, i + offset))


def struct(dtype, *shape):
    return jax.ShapeDtypeStruct(shape, dtype)


def call(kernel, grid, in_specs, out_specs, out_shape, flops, scratch=(), collective=None):
    return pl.pallas_call(
        kernel,
        grid=(grid,),
        in_specs=in_specs,
        out_specs=out_specs,
        out_shape=out_shape,
        scratch_shapes=list(scratch),
        compiler_params=pltpu.CompilerParams(
            dimension_semantics=("arbitrary",), vmem_limit_bytes=VMEM_LIMIT,
            collective_id=collective, has_side_effects=collective is not None,
        ),
        cost_estimate=pl.CostEstimate(flops=flops, bytes_accessed=10 * 2**20, transcendentals=0),
    )


MESH = pl.DeviceIdType.MESH
ANY = pl.BlockSpec(memory_space=pl.ANY)


def take(array, index):
    return lax.dynamic_index_in_dim(array, index, 0, keepdims=False)


def flip(index, mask):
    bit = 1
    while bit <= mask:
        if mask & bit:
            index = index + bit - 2 * bit * ((index // bit) % 2)
        bit *= 2
    return index


def flip_by(index, mask, size):
    total = 0
    for bit in bits_of(size):
        ours, theirs = (index // bit) % 2, (mask // bit) % 2
        total = total + bit * (ours + theirs - 2 * ours * theirs)
    return total


def bits_of(size):
    return [1 << i for i in range(size.bit_length() - 1)]


def meet(partners):
    barrier = pltpu.get_barrier_semaphore()
    for axis, mask in partners:
        pl.semaphore_signal(
            barrier, inc=1, device_id={axis: flip(lax.axis_index(axis), mask)}, device_id_type=MESH
        )
    pl.semaphore_wait(barrier, len(partners))


class Sems:
    def __init__(self, send, recv, local):
        self.send, self.recv, self.local = send, recv, local
        self.remote_used = self.local_used = 0

    def remote(self, src, dst, axis, mask):
        i = self.remote_used
        self.remote_used += 1
        return pltpu.make_async_remote_copy(
            src_ref=src, dst_ref=dst, send_sem=self.send.at[i], recv_sem=self.recv.at[i],
            device_id={axis: flip(lax.axis_index(axis), mask)}, device_id_type=MESH,
        )

    def copy(self, src, dst):
        i = self.local_used
        self.local_used += 1
        return pltpu.make_async_copy(src, dst, self.local.at[i])


def sem_shapes(remote, local):
    dma = pltpu.SemaphoreType.DMA
    return [dma((remote,)), dma((remote,)), dma((max(local, 1),))]


def start_all(copies):
    for copy in copies:
        copy.start()


def wait_all(copies):
    for copy in copies:
        copy.wait()


class Gather:
    def __init__(self, sizes, shards, place, sems, order):
        self.sizes, self.shards, self.place, self.sems = sizes, shards, place, sems
        self.pieces = order
        self.me, self.me_rep = lax.axis_index("fsdp"), lax.axis_index("rep")
        self.pending = []

    def part(self, ref, pieces, n):
        width = ref.shape[-1] // (self.sizes[1] * pieces)
        start = (self.me_rep * pieces + n) * width
        return ref.at[:, pl.ds(pl.multiple_of(start, 128), width)]

    def source(self, w, h):
        return self.shards[w] if h == 0 else self.place(w, flip(self.me, h))

    def start(self):
        self.held = [0]
        self.over = self.cross(self.far_bits()[0]) if self.far_bits() else []

    def far_bits(self):
        return list(reversed(bits_of(self.sizes[0])[1:]))

    def cross(self, bit):
        over = []
        for w, pieces, n in self.pieces:
            moved = [
                self.sems.remote(
                    self.part(self.source(w, h), pieces, n),
                    self.part(self.place(w, flip(self.me, h)), pieces, n), "fsdp", bit,
                )
                for h in self.held
            ]
            start_all(moved)
            over.append(moved)
        return over

    def pass_on(self, i, bit):
        w, pieces, n = self.pieces[i]
        for copy in self.over[i]:
            copy.wait_recv()
        self.pending += self.over[i]
        passed = []
        for mask in range(1, self.sizes[1]):
            for h in self.held:
                here = self.part(self.place(w, flip(self.me, h ^ bit)), pieces, n)
                passed.append(self.sems.remote(here, here, "rep", mask))
        start_all(passed)
        self.pending += passed
        return passed

    def events(self, lag=2):
        bits = self.far_bits()
        count = len(self.pieces)
        for bit in bits[:-1]:
            passed = [self.pass_on(i, bit) for i in range(count)]
            self.held = self.held + [h ^ bit for h in self.held]
            for copies in passed:
                for copy in copies:
                    copy.wait_recv()
            self.over = self.cross(bits[bits.index(bit) + 1])
        end = {w: i for i, (w, _, _) in enumerate(self.pieces)}
        passed, near_held = [], self.held + [h ^ bit for bit in bits[-1:] for h in self.held]
        for i in range(count + lag):
            if i < count:
                if bits:
                    passed.append(self.pass_on(i, bits[-1]))
                yield None
            for w, last in end.items():
                if last == i - lag:
                    if bits:
                        for j, (other, _, _) in enumerate(self.pieces):
                            if other == w:
                                for copy in passed[j]:
                                    copy.wait_recv()
                    yield w, self.near(w, near_held)

    def near(self, w, held):
        copies = [self.sems.remote(self.source(w, h), self.place(w, flip(self.me, h)), "fsdp", 1) for h in held]
        start_all(copies)
        return copies

    @staticmethod
    def count(sizes, order, weights):
        held, copies = 1, 0
        for _ in bits_of(sizes[0])[1:]:
            copies += len(order) * held * sizes[1]
            held *= 2
        return copies + weights * held


PASSED = (0, 1, 2, 4, 6, 6, 6)
CROSSED = (4, 5)


class LateGather:
    def __init__(self, sizes, shards, wholes, sems):
        fsdp, rep, _ = sizes
        me, me_rep = lax.axis_index("fsdp"), lax.axis_index("rep")
        place = lambda w, q: shard_of(wholes[w], shards[w].shape[0], q)
        self.own = [sems.copy(shards[w], place(w, me)) for w in range(2)]
        self.far, self.passed, self.near = [], [], [[], []]
        for w in range(2):
            fits = shards[w].shape[-1] % (rep * 3 * 128) == 0
            pieces = 3 if fits else 1
            width = shards[w].shape[-1] // (rep * pieces)
            for n in range(pieces if fsdp > 2 else 0):
                cols = pl.ds(pl.multiple_of((me_rep * pieces + n) * width, 128), width)
                self.far.append(sems.remote(shards[w].at[:, cols], place(w, me).at[:, cols], "fsdp", 2))
                here = place(w, flip(me, 2)).at[:, cols]
                self.passed.append([sems.remote(here, here, "rep", mask) for mask in range(1, rep)])
            for h in range(0, fsdp, 2):
                src = shards[w] if h == 0 else place(w, flip(me, h))
                self.near[w].append(sems.remote(src, place(w, flip(me, h)), "fsdp", 1))
        self.pieces = len(self.far) // 2
        self.count = len(self.far)

    @staticmethod
    def copies(sizes):
        return 2 * (3 * sizes[1] + sizes[0] // 2)

    def pass_on(self, i):
        self.far[i].wait_recv()
        start_all(self.passed[i])

    def cross_core(self, w):
        for copies in self.passed[w * self.pieces : (w + 1) * self.pieces]:
            for copy in copies:
                copy.wait_recv()
        start_all(self.near[w])

    def advance(self, step):
        upto = lambda n: min(n, self.count)
        for i in range(upto(PASSED[step - 1]), upto(PASSED[step])):
            self.pass_on(i)
        for w in range(2):
            if step == CROSSED[w]:
                self.cross_core(w)

    def finish(self, w):
        wait_all(self.own[w : w + 1])
        for i in range(w * self.pieces, (w + 1) * self.pieces):
            self.far[i].wait_send()
            for copy in self.passed[i]:
                copy.wait_send()
        wait_all(self.near[w])


def gather_order(sizes, shards):
    fits = lambda w, n: shards[w].shape[-1] % (sizes[1] * n * 128) == 0
    split = lambda w, n: n if fits(w, n) else 1
    order = []
    for w, n in ((0, 1), (1, 3), (2, 3), (4, 3), (3, 3)):
        if w >= len(shards):
            continue
        n = split(w, n)
        order += [(w, n, i) for i in range(n)]
    return order


def enter_kernel(sizes, count, tokens, *refs):
    fsdp, rep, seq = sizes
    refs = list(refs)
    pop = lambda n: [refs.pop(0) for _ in range(n)]
    shards = pop(count)
    (x_out,) = pop(1)
    fulls = pop(count)
    (bounce_x,) = pop(1)
    bounces = pop(count)
    sems = Sems(*refs)
    me, me_seq = lax.axis_index("fsdp"), lax.axis_index("seq")
    into = [sems.copy(tokens.at[me_seq], bounce_x)] + [sems.copy(shards[w], bounces[w]) for w in range(count)]
    outof = [sems.copy(bounce_x, x_out.at[0])] + [sems.copy(bounces[w], fulls[w].at[me]) for w in range(count)]
    gather = Gather(sizes, shards, lambda w, q: fulls[w].at[q], sems, gather_order(sizes, shards))
    start_all(into)
    meet(all_partners(sizes))
    blocks = [sems.remote(tokens.at[flip(me_seq, k)], x_out.at[k], "seq", k) for k in range(1, seq)]
    start_all(blocks)
    gather.start()
    last = []
    for event in gather.events():
        if event:
            last += event[1]
    wait_all(into)
    start_all(outof)
    for copy in gather.pending:
        copy.wait_send()
    wait_all(last)
    wait_all(blocks)
    wait_all(outof)


def enter(sizes, tokens, shards):
    fsdp = sizes[0]
    count = len(shards)
    hbm = lambda shape: struct(bf16, *shape)
    copies = sizes[2] - 1 + Gather.count(sizes, gather_order(sizes, shards), count)
    return pl.pallas_call(
        functools.partial(enter_kernel, sizes, count),
        in_specs=[ANY] * (1 + count),
        out_specs=[ANY] * (1 + count),
        out_shape=[hbm(tokens.shape)] + [hbm((fsdp,) + s.shape) for s in shards],
        scratch_shapes=[pltpu.VMEM(tokens.shape[1:], bf16)]
        + [pltpu.VMEM(s.shape, bf16) for s in shards]
        + sem_shapes(copies, 2 * (1 + count)),
        compiler_params=pltpu.CompilerParams(collective_id=0, has_side_effects=True),
    )(tokens, *shards)


def turn(row):
    n = row.shape[1]
    diagonal = lax.broadcasted_iota(jnp.int32, (n, n), 0) == lax.broadcasted_iota(jnp.int32, (n, n), 1)
    return jnp.sum(jnp.where(diagonal, row, 0), axis=1, keepdims=True)


def enter_project_kernel(sizes, count, tokens, segments, *refs):
    fsdp, rep, seq = sizes
    refs = list(refs)
    pop = lambda n: [refs.pop(0) for _ in range(n)]
    shards = pop(count)
    x_out, a_out, qkv_out, cos_out, sin_out, marks_out, row_out, gains_out, wq_out = pop(9)
    fulls = [None, None] + pop(count - 2)
    xs, a, qkv, wq, gains = pop(5)
    bounces = pop(count)
    sems = Sems(*refs)
    me, me_seq = lax.axis_index("fsdp"), lax.axis_index("seq")
    shard_rows, rows = shards[1].shape[0], xs.shape[1]
    columns = wq.shape[1]

    def place(w, q):
        if w == 0:
            return gains.at[q]
        if w == 1:
            return wq.at[pl.ds(pl.multiple_of(q * shard_rows, 16), shard_rows)]
        return fulls[w].at[q]

    own = sems.copy(tokens.at[me_seq], xs.at[0])
    into = [sems.copy(shards[w], place(w, me) if w < 2 else bounces[w - 2]) for w in range(count)]
    outof = [sems.copy(bounces[w - 2], place(w, me)) for w in range(2, count)]
    blocks = [sems.remote(tokens.at[flip(me_seq, k)], xs.at[k], "seq", k) for k in range(1, seq)]
    stores = [
        [sems.copy(src.at[k], dst.at[k]) for src, dst in ((xs, x_out), (a, a_out), (qkv, qkv_out))] for k in range(seq)
    ]
    keep = sems.copy(wq, wq_out)
    gather = Gather(sizes, shards, place, sems, gather_order(sizes, shards))
    own.start()
    start_all(into)
    meet(all_partners(sizes))
    gather.start()
    start_all(blocks)

    lane = lax.broadcasted_iota(jnp.int32, (1, PAIR), 1)
    rate = jnp.exp((lane % (HDIM // 2)).astype(f32) * (-2.0 * math.log(THETA) / HDIM))
    sign = jnp.where(lane_halves((1, PAIR)), -1.0, 1.0)
    batch = segments.shape[1]

    def own_segments(block):
        at = pl.multiple_of(block * rows, 128)
        return segments[me_seq // batch, pl.ds(me_seq % batch, 1), pl.ds(at, rows)]

    @pl.loop(0, seq)
    def _(k):
        block = flip_by(me_seq, k, seq)
        piece = pl.ds(pl.multiple_of(k * rows, 128), rows)
        row = own_segments(block)
        column = turn(row)
        earlier = jnp.zeros((rows, 1), jnp.int32)
        for other in range(seq):
            earlier += jnp.sum((own_segments(other) < column).astype(jnp.int32), axis=1, keepdims=True)
        index = block * rows + lax.broadcasted_iota(jnp.int32, (rows, 1), 0)
        angles = (index - earlier).astype(f32) * rate
        cos_out[piece, :] = jnp.cos(angles)
        sin_out[piece, :] = jnp.sin(angles) * sign
        marks_out[piece, :] = column
        row_out[:, piece] = row

    def project(k):
        if k == 0:
            own.wait()
        else:
            blocks[k - 1].wait()
        piece = slice(k * rows, (k + 1) * rows)
        unit, _ = normalize(xs[k].astype(f32))
        low = (unit * gains_out[0:1, :]).astype(bf16)
        a[k] = low
        cosine, sine = cos_out[piece, :], sin_out[piece, :]

        @pl.loop(0, 2 * D // WIDE)
        def _(i):
            at = pl.multiple_of(i * WIDE, WIDE)
            part = dot_nn(low, wq[:, pl.ds(at, WIDE)])
            scale = jnp.where(at < D, QUERY_SCALE, 1.0)
            for half in range(0, WIDE, PAIR):
                value = rotate_pair(part[:, half : half + PAIR], cosine, sine) * scale
                qkv[k, :, pl.ds(at + half, PAIR)] = value.astype(bf16)

        qkv[k, :, 2 * D :] = dot_nn(low, wq[:, 2 * D :]).astype(bf16)
        start_all(stores[k])

    last, queue, since = {}, list(range(seq)), 0
    for event in gather.events():
        if event:
            last[event[0]] = event[1]
            if event[0] == 1:
                for copy in into[:2] + last[0] + last[1]:
                    copy.wait()
                keep.start()
                total = gains[0, :2, :].astype(f32)
                for q in range(1, fsdp):
                    total = total + gains[q, :2, :].astype(f32)
                gains_out[...] = total
                wait_all(into[2:])
                start_all(outof)
                project(queue.pop(0))
        elif 1 in last:
            since += 1
            if since % 2 == 0 and len(queue) > 1:
                project(queue.pop(0))
    for k in queue:
        project(k)
    for copy in gather.pending:
        copy.wait_send()
    for w in range(2, count):
        wait_all(last[w])
    wait_all(outof)
    for group in stores:
        wait_all(group)
    keep.wait()


def enter_project(sizes, tokens, segments, shards):
    fsdp, rep, seq = sizes
    count, rows = len(shards), tokens.shape[1]
    length, columns = seq * rows, shards[1].shape[1]
    vmem = pl.BlockSpec(memory_space=pltpu.VMEM)
    copies = seq - 1 + Gather.count(sizes, gather_order(sizes, shards), count)
    return pl.pallas_call(
        functools.partial(enter_project_kernel, sizes, count),
        in_specs=[ANY, vmem] + [ANY] * count,
        out_specs=[ANY] * 3 + [vmem] * 5 + [ANY] * (count - 1),
        out_shape=[struct(bf16, seq, rows, D), struct(bf16, seq, rows, D), struct(bf16, seq, rows, columns),
                   struct(f32, length, PAIR), struct(f32, length, PAIR), struct(jnp.int32, length, 1),
                   struct(jnp.int32, 1, length), struct(f32, 2, D), struct(bf16, D, columns)]
        + [struct(bf16, fsdp, *s.shape) for s in shards[2:]],
        scratch_shapes=[pltpu.VMEM((seq, rows, D), bf16), pltpu.VMEM((seq, rows, D), bf16),
                        pltpu.VMEM((seq, rows, columns), bf16), pltpu.VMEM((D, columns), bf16),
                        pltpu.VMEM((fsdp,) + shards[0].shape, bf16)]
        + [pltpu.VMEM(s.shape, bf16) for s in shards[2:]] + [pltpu.VMEM((16, 128), bf16)] * 2
        + sem_shapes(copies, 2 + count + count - 2 + 3 * seq),
        compiler_params=pltpu.CompilerParams(
            collective_id=4, has_side_effects=True, vmem_limit_bytes=VMEM_LIMIT
        ),
    )(tokens, segments, *shards)


def add_into(total, term):
    rows = total.shape[0]
    height = 48 if rows % 48 == 0 else rows

    @pl.loop(0, rows // height)
    def _(i):
        at = pl.ds(pl.multiple_of(i * height, 16), height) if height < rows else pl.ds(0, rows)
        total[at, :] = (total[at, :].astype(f32) + term[at, :].astype(f32)).astype(bf16)


class Reducer:
    def __init__(self, parts_shape, sizes, order):
        self.fsdp, self.rows, self.cols = parts_shape
        self.steps = []
        held, rows, cols = list(range(self.fsdp)), self.rows, self.cols
        row_at, col_at = [], []
        for axis, bit in order:
            step = dict(axis=axis, bit=bit, row_at=list(row_at), col_at=list(col_at), rows=rows, cols=cols)
            if axis == "fsdp":
                step["send"] = [j for j in held if j & bit]
                held = [j for j in held if not j & bit]
                step["keep"] = held
                step["shape"] = (len(held), rows, cols)
                step["split"] = None
            else:
                step["keep"] = step["send"] = held
                if (axis, bit) == order[-1]:
                    step["split"] = "none"
                elif (rows // 2) % 16 == 0:
                    rows //= 2
                    row_at = row_at + [(axis, bit, rows)]
                    step["split"] = "rows"
                elif (cols // 2) % 128 == 0:
                    cols //= 2
                    col_at = col_at + [(axis, bit, cols)]
                    step["split"] = "cols"
                else:
                    step["split"] = "none"
                step["shape"] = (len(held), rows, cols)
            self.steps.append(step)
        self.down = len(self.steps)
        for step in reversed(self.steps[: self.down]):
            if step["split"] in ("rows", "cols"):
                self.steps.append(dict(step, up=True))

    @staticmethod
    def offset(terms, align, last=None):
        total = 0
        for i, (axis, bit, extent) in enumerate(terms):
            half = (lax.axis_index(axis) // bit) % 2
            if last == i:
                half = 1 - half
            total = total + half * extent
        return total if isinstance(total, int) else pl.multiple_of(total, align)

    def region(self, step, after, other=False):
        row_at, col_at, rows, cols = step["row_at"], step["col_at"], step["rows"], step["cols"]
        row_last = col_last = None
        if after:
            if step["split"] == "rows":
                rows //= 2
                row_at = row_at + [(step["axis"], step["bit"], rows)]
                row_last = len(row_at) - 1 if other else None
            elif step["split"] == "cols":
                cols //= 2
                col_at = col_at + [(step["axis"], step["bit"], cols)]
                col_last = len(col_at) - 1 if other else None
        return (
            pl.ds(self.offset(row_at, 16, row_last), rows),
            pl.ds(self.offset(col_at, 128, col_last), cols),
        )

    def scratch(self, first, last):
        return [pltpu.VMEM(s["shape"], bf16) for s in self.steps[first:last] if "up" not in s]

    def copies(self, first, last):
        return sum(1 if "up" in s else len(s["send"]) for s in self.steps[first:last])

    def bind(self, parts, lands, sems, first, last, final=None):
        self.parts, self.sems, self.final = parts, sems, final
        self.lands, self.moves = {}, {}
        lands = list(lands)
        for s in range(first, last):
            step = self.steps[s]
            moves = []
            if "up" in step:
                there = final.at[self.region(step, True)]
                moves.append(sems.remote(there, there, step["axis"], step["bit"]))
            else:
                land = self.lands[s] = lands.pop(0)
                for i, j in enumerate(step["send"]):
                    fsdp = step["axis"] == "fsdp"
                    src = self.parts(j).at[self.region(step, not fsdp, not fsdp)]
                    moves.append(sems.remote(src, land.at[i], step["axis"], step["bit"]))
            self.moves[s] = moves

    def start(self, s):
        if s == self.down:
            region = self.region(self.steps[s - 1], True)
            self.final[region] = self.parts(0)[region]
        start_all(self.moves.get(s, []))

    def finish(self, s):
        step = self.steps[s]
        self.finish_step(s, step)
        if s + 1 == len(self.steps) == self.down and self.final is not None:
            self.final[...] = self.parts(0)[...]

    def finish_step(self, s, step):
        for i, move in enumerate(self.moves[s]):
            move.wait()
            if "up" not in step:
                j = step["keep"][i]
                ref = self.parts(j)
                add_into(ref.at[self.region(step, True)], self.lands[s].at[i])


def give_back(slots, home, bounce, sems):
    me = lax.axis_index("seq")
    seq = slots.shape[0]
    return (
        sems.copy(slots.at[0], bounce),
        sems.copy(bounce, home.at[me]),
        [sems.remote(slots.at[k], home.at[me], "seq", k) for k in range(1, seq)],
    )


def body(sizes, tokens, segments, positions, gain_attn, w_qkv, w_out, gain_mlp, w_in, w_mlp_out, cotangent):
    fsdp, rep, seq = sizes
    micro, batch, rows, _ = tokens.shape
    assert micro * batch == seq and rows % TILE == 0
    length = seq * rows
    me_seq, me_fsdp = lax.axis_index("seq"), lax.axis_index("fsdp")

    own_gains = jnp.zeros((16, D), bf16)
    own_gains = lax.dynamic_update_slice(own_gains, jnp.stack([gain_attn, gain_mlp]), (0, me_fsdp * (D // fsdp)))
    shards = [own_gains, w_qkv, w_out, w_mlp_out, w_in]
    tiles, pairs = length // TILE, HEADS // 2
    late = fsdp in (2, 4) and pairs >= 6 and flat(D // fsdp) and flat(FF // fsdp)
    if (D // fsdp) % 16 == 0:
        x, a, qkv, cosine, sine, marks_column, marks_row, gains, wq, *rest = enter_project(
            sizes, tokens.reshape(seq, rows, D), segments, shards[:3] if late else shards
        )
        x, a, qkv = (v.reshape(length, -1) for v in (x, a, qkv))
        wo, *rest = (w.reshape(-1, w.shape[-1]) for w in rest)
        wm, wi = (w_mlp_out, w_in) if late else rest
    else:
        x, gains, wq, wo, wm, wi = enter(sizes, tokens.reshape(seq, rows, D), shards)
        x = x.reshape(length, D)
        gains = jnp.sum(gains[:, :2].astype(f32), axis=0)
        wq, wo, wm, wi = (w.reshape(-1, w.shape[-1]) for w in (wq, wo, wm, wi))

        marks = take(segments.reshape(seq, length), me_seq)
        place = jnp.arange(length, dtype=jnp.int32) - jnp.sum(
            (marks[None, :] < marks[:, None]).astype(jnp.int32), axis=1
        )
        slot_order = [me_seq ^ k for k in range(seq)]
        marks = jnp.concatenate([take(marks.reshape(seq, rows), s) for s in slot_order])
        place = jnp.concatenate([take(place.reshape(seq, rows), s) for s in slot_order])
        half = jnp.arange(0, HDIM, 2).astype(f32) / HDIM
        angles = place.astype(f32)[:, None] * jnp.exp(-half * math.log(THETA))
        cosine, sine = jnp.cos(angles), jnp.sin(angles)
        cosine = jnp.concatenate([cosine] * 4, -1)
        sine = jnp.concatenate([-sine, sine] * 2, -1)

        a, qkv = call(
            first_kernel, tiles,
            [rows_spec(D), whole_spec(2, D), whole_spec(D, 3 * D), rows_spec(PAIR), rows_spec(PAIR)],
            [rows_spec(D), rows_spec(3 * D)],
            [struct(bf16, length, D), struct(bf16, length, 3 * D)],
            2 * length * D * 3 * D,
        )(x, gains, wq, cosine, sine)
        marks_column, marks_row = marks[:, None], marks[None, :]

    vmem = pl.BlockSpec(memory_space=pltpu.VMEM)
    pair_at = lambda offset, lag, n: pl.BlockSpec(
        (length, PAIR), lambda i: (0, jnp.clip(i - lag, 0, n - 1) + offset)
    )
    prob_at = lambda lag: pl.BlockSpec((2, length, length), lambda i: (jnp.clip(i - lag, 0, pairs - 1), 0, 0))
    tile_at = lambda width, lag: pl.BlockSpec((TILE, width), lambda i: (jnp.clip(i - lag, 0, tiles - 1), 0))
    slots = struct(bf16, seq, rows, D)
    o, probs, inv, x1, b, m, slope, act, y, dy, *wholes = call(
        functools.partial(forward_kernel, sizes, pairs, late), pairs + tiles,
        [pair_at(0, 0, pairs), pair_at(pairs, 0, pairs), pair_at(2 * pairs, 0, pairs),
         whole_spec(length, 1), whole_spec(1, length), tile_at(D, pairs), whole_spec(2, D)] + [ANY] * 4,
        [pair_at(0, 0, pairs), prob_at(0), pair_at(0, 0, pairs), tile_at(D, pairs), tile_at(D, pairs)]
        + [tile_at(FF, pairs)] * 3 + [tile_at(D, pairs), ANY] + [ANY] * (2 * late),
        [struct(bf16, length, D), struct(bf16, HEADS, length, length), struct(f32, length, D),
         struct(f32, length, D), struct(bf16, length, D), struct(bf16, length, FF),
         struct(bf16, length, FF), struct(bf16, length, FF), struct(bf16, length, D), slots]
        + [struct(bf16, D, 2 * FF), struct(bf16, FF, D)] * late,
        16 * length * length * D,
        [pltpu.VMEM((length, D), bf16), pltpu.VMEM((D, D), bf16), pltpu.VMEM((D, 2 * FF), bf16), pltpu.VMEM((FF, D), bf16),
         pltpu.VMEM((rows, D), bf16)] + sem_shapes(seq - 1 + LateGather.copies(sizes) * late, 5 + 2 * late), 1,
    )(qkv, qkv, qkv, marks_column, marks_row, x, gains, wo, wi, wm, cotangent.reshape(seq, rows, D))

    if late:
        wi, wm = wholes
    reducers, early = early_reducers(sizes)
    whole = late_reducers(sizes)
    own_shard = lambda r: struct(bf16, r.rows, r.cols)
    full_shard = lambda r: pltpu.VMEM((fsdp * r.rows, r.cols) if flat(r.rows) else (fsdp, r.rows, r.cols), bf16)
    odd = (FF // fsdp) % 16 or (D // fsdp) % 16
    wide = pltpu.VMEM((FF, FF) if odd else (8, 128), f32)
    dx1, dgain_two, dq, dk, dv, block_out, *sums = call(
        functools.partial(backward_kernel, sizes, tiles), tiles + 1 + pairs,
        [tile_at(D, 0), tile_at(FF, 0), tile_at(FF, 0), whole_spec(2, D)]
        + [pair_at(n * pairs, tiles + 1, pairs) for n in range(3)]
        + [pair_at(0, tiles + 1, pairs), pair_at(0, tiles + 1, pairs)] + [ANY] * 11,
        [tile_at(D, 0), whole_spec(1, D)] + [pair_at(0, tiles + 1, pairs)] * 3 + [ANY] * (1 + len(reducers)),
        [struct(f32, length, D), struct(f32, 1, D)] + [struct(bf16, length, D)] * 3 + [slots]
        + [own_shard(r) for r in reducers],
        32 * length * length * D,
        [pltpu.VMEM((D, D), bf16), pltpu.VMEM((D, 2 * FF), bf16), pltpu.VMEM((FF, D), bf16),
         pltpu.VMEM((length, FF), bf16)] + [pltpu.VMEM((length, D), bf16)] * 3
        + [pltpu.VMEM((length, 2 * FF), bf16), pltpu.VMEM((length, D), bf16), pltpu.VMEM((length, D), bf16),
           wide, pltpu.VMEM((rows, D), bf16),
           pltpu.VMEM((2, 2, length, length), bf16)] + [pltpu.VMEM((length, PAIR), f32)] * 2
        + [full_shard(r) for r in reducers] + [pltpu.VMEM((reducers[0].rows, reducers[0].cols), bf16)]
        + [land for r, e in zip(reducers, early) for land in r.scratch(0, e)]
        + sem_shapes(seq - 1 + sum(r.copies(0, e) for r, e in zip(reducers, early)), 13 + len(reducers)), 2,
    )(x1, slope, act, gains, qkv, qkv, qkv, o, inv, probs, cosine, sine,
      wo, wi, wm, m, dy.reshape(length, D), b, o, y.reshape(seq, rows, D))

    hops = sum(len(bits_of(n)) for n in sizes)
    shard = lambda n, width: struct(bf16, n // fsdp, width)
    finals = [shard(D, 2 * FF), shard(D, D), shard(D, 3 * D)]
    operands = [dq, a, dk, dv, wq, x, dx1]
    grad_mlp, *sums = sums
    reducers, early = reducers[1:], early[1:]
    input_grad, grad_in, grad_out, grad_qkv, dgains = pl.pallas_call(
        functools.partial(leave_kernel, sizes),
        in_specs=[vmem] * 2 + [ANY] * (len(operands) + len(reducers)),
        out_specs=[ANY] * 4 + [vmem],
        out_shape=[slots] + finals + [struct(f32, 8, D)],
        scratch_shapes=[pltpu.VMEM(v.shape, v.dtype) for v in operands]
        + [pltpu.VMEM((seq, rows, D), bf16), wide]
        + [pltpu.VMEM(v.shape, v.dtype) for v in finals]
        + [pltpu.VMEM((r.rows, r.cols), bf16) for r in reducers]
        + [full_shard(r) for r in whole]
        + [land for r, e in zip(reducers, early) for land in r.scratch(e, len(r.steps))]
        + [land for r in whole for land in r.scratch(0, len(r.steps))]
        + [pltpu.VMEM((hops, 8, D), f32)]
        + sem_shapes(
            PIECES * (seq - 1) + hops + sum(r.copies(e, len(r.steps)) for r, e in zip(reducers, early))
            + sum(r.copies(0, len(r.steps)) for r in whole),
            1 + len(operands) + len(reducers) + len(finals),
        ),
        compiler_params=pltpu.CompilerParams(
            collective_id=3, has_side_effects=True, vmem_limit_bytes=VMEM_LIMIT
        ),
    )(gains, dgain_two, *operands, *sums)
    dgains = lax.dynamic_slice_in_dim(dgains, me_fsdp * (D // fsdp), D // fsdp, 1)
    return (
        block_out.reshape(tokens.shape),
        input_grad.astype(f32).reshape(tokens.shape),
        dgains[0],
        grad_qkv.astype(f32),
        grad_out.astype(f32),
        dgains[1],
        grad_in.astype(f32),
        grad_mlp.astype(f32),
    )


def solution(mesh):
    sizes = (mesh.shape["fsdp"], mesh.shape["rep"], mesh.shape["seq"])
    wide = P(None, ("rep", "fsdp"), "seq", None)
    placed = (
        wide, P(None, ("rep", "fsdp"), None), P(None, ("rep", "fsdp"), "seq"),
        P("fsdp"), P("fsdp", None), P("fsdp", None), P("fsdp"), P("fsdp", None), P("fsdp", None), wide,
    )
    return jax.shard_map(
        functools.partial(body, sizes),
        mesh=mesh,
        in_specs=placed,
        out_specs=(
            wide, wide, P("fsdp"), P("fsdp", None), P("fsdp", None), P("fsdp"), P("fsdp", None), P("fsdp", None),
        ),
        check_vma=False,
    )
```

profile of v0, /device:TPU:0, one launch (start us, length us, event | category | flops | bytes accessed | tf_op | source)
XLA Modules:
  0.0 252.4 jit_solution(2670660722706019282)
XLA Ops:
  0.6 0.7 stack.10
  1.3 0.7 stack.9
  2.0 0.5 dynamic_update_slice.3.refs_0_
  2.5 0.0 copy-start.5
  2.5 0.6 copy-done.5
  3.1 46.3 %shard_map.152 = (bf16[4,256,768]{2,1,0:T(8,128)(2,1)}, bf16[4,256,768]{2,1,0:T(8,128)(2,1)}, bf16[4,256,2304]{2,1,0:T(8,128)(2,1)}, f32[1024,128]{1,0:T(8,128)}...) custom-call(bf16[4,256,768]{2,1,0:T(8,128)(2,1)} %bitcast.17, ...), custom_call_target="tpu_custom_call" | custom-call | tf_op jit(solution)/shard_map/pallas_call | solution.py:1048
  49.3 48.0 %shard_map.153 = (bf16[1024,768]{1,0:T(8,128)(2,1)}, bf16[12,1024,1024]{2,1,0:T(8,128)(2,1)}, f32[1024,768]{1,0:T(8,128)}, f32[1024,768]{1,0:T(8,128)}, bf16[102...) custom-call(bf16[1024,2304]{1,0:T(8,128)(2,1)} %bitcast.21, ...), custom_call_target="tpu_custom_call" | custom-call | flops 12884901888 | bytes 10485760 | tf_op jit(solution)/shard_map/pallas_call | solution.py:1248
  97.4 71.1 %shard_map.154 = (f32[1024,768]{1,0:T(8,128)}, f32[1,768]{1,0:T(1,128)}, bf16[1024,768]{1,0:T(8,128)(2,1)}, bf16[1024,768]{1,0:T(8,128)(2,1)}, bf16[1024,768]{1,...) custom-call(f32[1024,768]{1,0:T(8,128)} %get-tuple-element.51.x1_ref, ...), custom_call_target="tpu_custom_call" | custom-call | flops 25769803776 | bytes 10485760 | tf_op jit(solution)/shard_map/pallas_call | solution.py:1271
  168.4 73.3 %shard_map.155 = (bf16[4,256,768]{2,1,0:T(8,128)(2,1)}, bf16[192,2304]{1,0:T(8,128)(2,1)}, bf16[192,768]{1,0:T(8,128)(2,1)}, bf16[192,2304]{1,0:T(8,128)(2,1)}, f32[8,768]{1,0:T(8,128)}) custom-call(f32[2,768]{1,0:T(2,128)} %get-tuple-element.49.gain_ref, f32[1,768]{1,0:T(1,128)} %get-tuple-element.66.other_gain_ref, ...), custom_call_target="tpu_custom_call" | custom-call | tf_op jit(solution)/shard_map/pallas_call | solution.py:1297
  241.8 0.0 copy-start.2
  241.8 3.4 %convert.1 = f32[2,2,256,768]{3,2,1,0:T(8,128)} convert(bf16[2,2,256,768]{3,2,1,0:T(8,128)(2,1)} %bitcast.18) | non-fusion elementwise | flops 786432 | bytes 4718592 | tf_op jit(solution)/shard_map/reshape | solution.py:1322
  245.2 0.0 copy-start.1
  245.2 0.0 copy-done.2
  245.2 1.3 convert_element_type.13
  246.6 0.0 copy-start.4
  246.6 0.2 copy-done.1
  246.7 1.3 convert_element_type.15
  248.1 0.0 copy-done.4
  248.1 0.9 convert_element_type.14
  248.9 1.4 fusion
  250.3 0.0 copy-done.3
  250.3 1.0 convert_element_type.16
  251.3 0.0 copy-done
  251.3 1.1 copy.19
  (4 shorter events, 0.0 us)
Async XLA Ops:
  2.5 0.6 copy-start.5
  241.8 3.4 %copy-start.2 = (bf16[192,2304]{1,0:T(8,128)(2,1)S(1)}, bf16[192,2304]{1,0:T(8,128)(2,1)}, u32[]{:S(2)}) copy-start(bf16[192,2304]{1,0:T(8,128)(2,1)} %get-tuple-element.78) | copy-start | bytes 2654212
  245.2 1.5 copy-start.1
  246.6 1.5 copy-start.4
  246.7 3.6 %copy-start.3 = (bf16[288,768]{1,0:T(8,128)(2,1)S(1)}, bf16[288,768]{1,0:T(8,128)(2,1)}, u32[]{:S(2)}) copy-start(bf16[288,768]{1,0:T(8,128)(2,1)} %get-tuple-element.81) | copy-start | bytes 1327108
  248.0 3.3 %copy-start = (bf16[4,256,768]{2,1,0:T(8,128)(2,1)S(1)}, bf16[4,256,768]{2,1,0:T(8,128)(2,1)}, u32[]{:S(2)}) copy-start(bf16[4,256,768]{2,1,0:T(8,128)(2,1)} %get-tuple-element.65) | copy-start | bytes 4718596
where the time goes:
time: 253 us; the launch traced here: 252 us
  Pallas kernels  239 us (94%)
  other arithmetic  7.89 us (3%)
  local copies, waits for them, and re-layouts  5.14 us (2%)
    pallas_call x1, Pallas kernels, body(): pl.pallas_call(functools.partial(leave_kernel, sizes), in_specs=[vmem] *...  73.3 us
    pallas_call x1, Pallas kernels, body(): call(functools.partial(backward_kernel, sizes, tiles), tiles + 1 + pairs,...  71.1 us
    pallas_call x1, Pallas kernels, body(): call(functools.partial(forward_kernel, sizes, pairs, late), pairs + tiles...  48 us
    pallas_call x1, Pallas kernels, enter_project(): pl.pallas_call(functools.partial(enter_project_kernel, sizes, count), in_...  46.3 us

commit v1 on v0

--- a/solution.py
+++ b/solution.py
@@ -576,24 +576,25 @@
     advance(whole[1:2], 1)
     advance(out, early[2] + 1)
     send_piece()
+    hop = 0
     for s in range(2, across):
         advance(whole[:1], s)
+        advance_gains(hop)
         advance(whole[2:], s - 1)
         advance(whole[1:2], s)
         send_piece()
+        hop += 1
     advance(whole[2:], across - 1)
+    advance_gains(hop)
     send_piece()
-    i = 0
     for s in range(across, last):
         for reducer in whole:
             advance([reducer], s)
             send_piece()
-        for _ in range(2):
-            advance_gains(i)
-            i += 1
-    while i < len(hops):
+        hop += 1
+        advance_gains(hop)
+    for i in range(hop + 1, len(hops)):
         advance_gains(i)
-        i += 1
     send_piece(len(ready))
     for s in range(early[0] + 1, len(halves[0].steps)):
         advance(halves, s)

time: 253 us -> 247 us (0.976)
  Pallas kernels: 239 us -> 233 us
    pallas_call x1, Pallas kernels: 73.3 us -> 67.4 us  [body(): pl.pallas_call(functools.partial(leave_kernel, sizes), in_specs=[vmem] *...]
where the time goes in v1:
time: 247 us
  Pallas kernels  233 us (94%)
  other arithmetic  7.89 us (3%)
  local copies, waits for them, and re-layouts  5.14 us (2%)
    pallas_call x1, Pallas kernels, body(): call(functools.partial(backward_kernel, sizes, tiles), tiles + 1 + pairs,...  71.1 us
    pallas_call x1, Pallas kernels, body(): pl.pallas_call(functools.partial(leave_kernel, sizes), in_specs=[vmem] *...  67.4 us
    pallas_call x1, Pallas kernels, body(): call(functools.partial(forward_kernel, sizes, pairs, late), pairs + tiles...  48 us
    pallas_call x1, Pallas kernels, enter_project(): pl.pallas_call(functools.partial(enter_project_kernel, sizes, count), in_...  46.3 us

profile of v1, /device:TPU:0, one launch (start us, length us, event | category | flops | bytes accessed | tf_op | source)
XLA Modules:
  0.0 246.5 jit_solution(16036438029199848542)
XLA Ops:
  0.6 0.7 stack.10
  1.3 0.7 stack.9
  2.0 0.5 dynamic_update_slice.3.refs_0_
  2.5 0.0 copy-start.5
  2.5 0.6 copy-done.5
  3.1 46.3 %shard_map.152 = (bf16[4,256,768]{2,1,0:T(8,128)(2,1)}, bf16[4,256,768]{2,1,0:T(8,128)(2,1)}, bf16[4,256,2304]{2,1,0:T(8,128)(2,1)}, f32[1024,128]{1,0:T(8,128)}...) custom-call(bf16[4,256,768]{2,1,0:T(8,128)(2,1)} %bitcast.17, ...), custom_call_target="tpu_custom_call" | custom-call | tf_op jit(solution)/shard_map/pallas_call | solution.py:1049
  49.3 48.0 %shard_map.153 = (bf16[1024,768]{1,0:T(8,128)(2,1)}, bf16[12,1024,1024]{2,1,0:T(8,128)(2,1)}, f32[1024,768]{1,0:T(8,128)}, f32[1024,768]{1,0:T(8,128)}, bf16[102...) custom-call(bf16[1024,2304]{1,0:T(8,128)(2,1)} %bitcast.21, ...), custom_call_target="tpu_custom_call" | custom-call | flops 12884901888 | bytes 10485760 | tf_op jit(solution)/shard_map/pallas_call | solution.py:1249
  97.4 71.1 %shard_map.154 = (f32[1024,768]{1,0:T(8,128)}, f32[1,768]{1,0:T(1,128)}, bf16[1024,768]{1,0:T(8,128)(2,1)}, bf16[1024,768]{1,0:T(8,128)(2,1)}, bf16[1024,768]{1,...) custom-call(f32[1024,768]{1,0:T(8,128)} %get-tuple-element.51.x1_ref, ...), custom_call_target="tpu_custom_call" | custom-call | flops 25769803776 | bytes 10485760 | tf_op jit(solution)/shard_map/pallas_call | solution.py:1272
  168.4 67.4 %shard_map.155 = (bf16[4,256,768]{2,1,0:T(8,128)(2,1)}, bf16[192,2304]{1,0:T(8,128)(2,1)}, bf16[192,768]{1,0:T(8,128)(2,1)}, bf16[192,2304]{1,0:T(8,128)(2,1)}, f32[8,768]{1,0:T(8,128)}) custom-call(f32[2,768]{1,0:T(2,128)} %get-tuple-element.49.gain_ref, f32[1,768]{1,0:T(1,128)} %get-tuple-element.66.other_gain_ref, ...), custom_call_target="tpu_custom_call" | custom-call | tf_op jit(solution)/shard_map/pallas_call | solution.py:1298
  235.9 0.0 copy-start.2
  235.9 3.4 %convert.1 = f32[2,2,256,768]{3,2,1,0:T(8,128)} convert(bf16[2,2,256,768]{3,2,1,0:T(8,128)(2,1)} %bitcast.18) | non-fusion elementwise | flops 786432 | bytes 4718592 | tf_op jit(solution)/shard_map/reshape | solution.py:1323
  239.3 0.0 copy-start.1
  239.3 0.0 copy-done.2
  239.3 1.3 convert_element_type.13
  240.6 0.0 copy-start.4
  240.6 0.2 copy-done.1
  240.8 1.3 convert_element_type.15
  242.1 0.0 copy-done.4
  242.1 0.9 convert_element_type.14
  243.0 1.4 fusion
  244.4 0.0 copy-done.3
  244.4 1.0 convert_element_type.16
  245.4 0.0 copy-done
  245.4 1.1 copy.19
  (4 shorter events, 0.0 us)
Async XLA Ops:
  2.5 0.6 copy-start.5
  235.9 3.4 %copy-start.2 = (bf16[192,2304]{1,0:T(8,128)(2,1)S(1)}, bf16[192,2304]{1,0:T(8,128)(2,1)}, u32[]{:S(2)}) copy-start(bf16[192,2304]{1,0:T(8,128)(2,1)} %get-tuple-element.78) | copy-start | bytes 2654212
  239.3 1.5 copy-start.1
  240.6 1.5 copy-start.4
  240.8 3.6 %copy-start.3 = (bf16[288,768]{1,0:T(8,128)(2,1)S(1)}, bf16[288,768]{1,0:T(8,128)(2,1)}, u32[]{:S(2)}) copy-start(bf16[288,768]{1,0:T(8,128)(2,1)} %get-tuple-element.81) | copy-start | bytes 1327108
  242.1 3.3 %copy-start = (bf16[4,256,768]{2,1,0:T(8,128)(2,1)S(1)}, bf16[4,256,768]{2,1,0:T(8,128)(2,1)}, u32[]{:S(2)}) copy-start(bf16[4,256,768]{2,1,0:T(8,128)(2,1)} %get-tuple-element.65) | copy-start | bytes 4718596

commit v2 on v1

--- a/solution.py
+++ b/solution.py
@@ -607,6 +607,34 @@
         wait_all(blocks[k])
 
 
+def widen_kernel(count, *refs):
+    anys, outs, narrow = refs[:count], refs[count : 2 * count], refs[2 * count : 3 * count]
+    wide, sems = refs[3 * count : -1], refs[-1]
+    loads = [pltpu.make_async_copy(anys[i], narrow[i], sems.at[i]) for i in range(count)]
+    start_all(loads)
+    stores = []
+    for i in range(count):
+        loads[i].wait()
+        wide[i][...] = narrow[i][...].astype(wide[i].dtype)
+        stores.append(pltpu.make_async_copy(wide[i], outs[i], sems.at[count + i]))
+        stores[-1].start()
+    wait_all(stores)
+
+
+def widen(arrays, dtypes):
+    count = len(arrays)
+    return pl.pallas_call(
+        functools.partial(widen_kernel, count),
+        in_specs=[ANY] * count,
+        out_specs=[ANY] * count,
+        out_shape=[struct(t, *v.shape) for v, t in zip(arrays, dtypes)],
+        scratch_shapes=[pltpu.VMEM(v.shape, v.dtype) for v in arrays]
+        + [pltpu.VMEM(v.shape, t) for v, t in zip(arrays, dtypes)]
+        + [pltpu.SemaphoreType.DMA((2 * count,))],
+        compiler_params=pltpu.CompilerParams(vmem_limit_bytes=VMEM_LIMIT),
+    )(*arrays)
+
+
 def rows_spec(width):
     return pl.BlockSpec((TILE, width), lambda i: (i, 0))
 
@@ -1318,15 +1346,18 @@
         ),
     )(gains, dgain_two, *operands, *sums)
     dgains = lax.dynamic_slice_in_dim(dgains, me_fsdp * (D // fsdp), D // fsdp, 1)
+    input_grad, grad_qkv, grad_in, grad_mlp, grad_out, block_out = widen(
+        [input_grad, grad_qkv, grad_in, grad_mlp, grad_out, block_out], [f32] * 5 + [bf16]
+    )
     return (
         block_out.reshape(tokens.shape),
-        input_grad.astype(f32).reshape(tokens.shape),
+        input_grad.reshape(tokens.shape),
         dgains[0],
-        grad_qkv.astype(f32),
-        grad_out.astype(f32),
+        grad_qkv,
+        grad_out,
         dgains[1],
-        grad_in.astype(f32),
-        grad_mlp.astype(f32),
+        grad_in,
+        grad_mlp,
     )
 
 

time: 247 us -> 244 us (0.988)
  other arithmetic: 7.89 us -> 0.01 us
  Pallas kernels: 233 us -> 239 us
    pallas_call x0 -> x1, Pallas kernels: none -> 5.45 us  [widen(): pl.pallas_call(functools.partial(widen_kernel, count), in_specs=[ANY] * c...]
    convert_element_type x4 -> x0, other arithmetic: 4.47 us -> none  [the longest x1 1.32 us: body(): grad_qkv.astype(f32)]
    reshape x1 -> x0, other arithmetic: 3.41 us -> none  [body(): input_grad.astype(f32).reshape(tokens.shape)]
where the time goes in v2:
time: 244 us; the launch traced here: 243 us
  Pallas kernels  239 us (98%)
  local copies, waits for them, and re-layouts  3.82 us (2%)
    pallas_call x1, Pallas kernels, body(): call(functools.partial(backward_kernel, sizes, tiles), tiles + 1 + pairs,...  71.2 us
    pallas_call x1, Pallas kernels, body(): pl.pallas_call(functools.partial(leave_kernel, sizes), in_specs=[vmem] *...  67.6 us
    pallas_call x1, Pallas kernels, body(): call(functools.partial(forward_kernel, sizes, pairs, late), pairs + tiles...  48.1 us
    pallas_call x1, Pallas kernels, enter_project(): pl.pallas_call(functools.partial(enter_project_kernel, sizes, count), in_...  46.2 us
    pallas_call x1, Pallas kernels, widen(): pl.pallas_call(functools.partial(widen_kernel, count), in_specs=[ANY] * c...  5.45 us

profile of v2, /device:TPU:0, one launch (start us, length us, event | category | flops | bytes accessed | tf_op | source)
XLA Modules:
  0.0 243.1 jit_solution(1347011766216552491)
XLA Ops:
  0.6 0.7 stack.10
  1.3 0.7 stack.9
  2.0 0.5 dynamic_update_slice.3.refs_0_
  2.5 0.0 copy-start
  2.5 0.6 copy-done
  3.1 46.2 %shard_map.152 = (bf16[4,256,768]{2,1,0:T(8,128)(2,1)}, bf16[4,256,768]{2,1,0:T(8,128)(2,1)}, bf16[4,256,2304]{2,1,0:T(8,128)(2,1)}, f32[1024,128]{1,0:T(8,128)}...) custom-call(bf16[4,256,768]{2,1,0:T(8,128)(2,1)} %bitcast.15, ...), custom_call_target="tpu_custom_call" | custom-call | tf_op jit(solution)/shard_map/pallas_call | solution.py:1077
  49.3 48.1 %shard_map.153 = (bf16[1024,768]{1,0:T(8,128)(2,1)}, bf16[12,1024,1024]{2,1,0:T(8,128)(2,1)}, f32[1024,768]{1,0:T(8,128)}, f32[1024,768]{1,0:T(8,128)}, bf16[102...) custom-call(bf16[1024,2304]{1,0:T(8,128)(2,1)} %bitcast.18, ...), custom_call_target="tpu_custom_call" | custom-call | flops 12884901888 | bytes 10485760 | tf_op jit(solution)/shard_map/pallas_call | solution.py:1277
  97.4 71.2 %shard_map.154 = (f32[1024,768]{1,0:T(8,128)}, f32[1,768]{1,0:T(1,128)}, bf16[1024,768]{1,0:T(8,128)(2,1)}, bf16[1024,768]{1,0:T(8,128)(2,1)}, bf16[1024,768]{1,...) custom-call(f32[1024,768]{1,0:T(8,128)} %get-tuple-element.57.x1_ref, ...), custom_call_target="tpu_custom_call" | custom-call | flops 25769803776 | bytes 10485760 | tf_op jit(solution)/shard_map/pallas_call | solution.py:1300
  168.6 67.6 %shard_map.155 = (bf16[4,256,768]{2,1,0:T(8,128)(2,1)}, bf16[192,2304]{1,0:T(8,128)(2,1)}, bf16[192,768]{1,0:T(8,128)(2,1)}, bf16[192,2304]{1,0:T(8,128)(2,1)}, f32[8,768]{1,0:T(8,128)}) custom-call(f32[2,768]{1,0:T(2,128)} %get-tuple-element.51.gain_ref, f32[1,768]{1,0:T(1,128)} %get-tuple-element.71.other_gain_ref, ...), custom_call_target="tpu_custom_call" | custom-call | tf_op jit(solution)/shard_map/pallas_call | solution.py:1326
  236.2 5.5 %shard_map.156 = (f32[4,256,768]{2,1,0:T(8,128)}, f32[192,2304]{1,0:T(8,128)}, f32[192,2304]{1,0:T(8,128)}, f32[288,768]{1,0:T(8,128)}, f32[192,768]{1,0:T(8,128)}, /*index=5*/bf16[4,256,768]{2,1,0:T(8,128)(2,1)}) custom-call(bf16[4,256,768]{2,1,0:T(8,128)(2,1)} %get-tuple-element.81.refs_0_, bf16[192,2304]{1,0:T(8,128)(2,1)} %get-tuple-element.82.refs_1_, ...), custom_call_target="tpu_custom_call" | custom-call | tf_op jit(solution)/shard_map/pallas_call | solution.py:626
  241.7 1.4 fusion
  (2 shorter events, 0.0 us)
Async XLA Ops:
  2.5 0.6 copy-start

commit v3 on v2

--- a/solution.py
+++ b/solution.py
@@ -1025,14 +1025,13 @@
         a[k] = low
         cosine, sine = cos_out[piece, :], sin_out[piece, :]
 
-        @pl.loop(0, 2 * D // WIDE)
-        def _(i):
-            at = pl.multiple_of(i * WIDE, WIDE)
-            part = dot_nn(low, wq[:, pl.ds(at, WIDE)])
-            scale = jnp.where(at < D, QUERY_SCALE, 1.0)
+        for at in range(0, 2 * D, WIDE):
+            part = dot_nn(low, wq[:, at : at + WIDE])
             for half in range(0, WIDE, PAIR):
-                value = rotate_pair(part[:, half : half + PAIR], cosine, sine) * scale
-                qkv[k, :, pl.ds(at + half, PAIR)] = value.astype(bf16)
+                value = rotate_pair(part[:, half : half + PAIR], cosine, sine)
+                if at < D:
+                    value = value * QUERY_SCALE
+                qkv[k, :, at + half : at + half + PAIR] = value.astype(bf16)
 
         qkv[k, :, 2 * D :] = dot_nn(low, wq[:, 2 * D :]).astype(bf16)
         start_all(stores[k])

time: 244 us -> 242 us (level)
    pallas_call x1, Pallas kernels: 46.2 us -> 40.6 us  [enter_project(): pl.pallas_call(functools.partial(enter_project_kernel, sizes, count), in_...]
    pallas_call x1, Pallas kernels: 48.1 us -> 52.3 us  [body(): call(functools.partial(forward_kernel, sizes, pairs, late), pairs + tiles...]
where the time goes in v3:
time: 242 us
  Pallas kernels  238 us (98%)
  local copies, waits for them, and re-layouts  3.82 us (2%)
    pallas_call x1, Pallas kernels, body(): call(functools.partial(backward_kernel, sizes, tiles), tiles + 1 + pairs,...  71.1 us
    pallas_call x1, Pallas kernels, body(): pl.pallas_call(functools.partial(leave_kernel, sizes), in_specs=[vmem] *...  68 us
    pallas_call x1, Pallas kernels, body(): call(functools.partial(forward_kernel, sizes, pairs, late), pairs + tiles...  52.3 us
    pallas_call x1, Pallas kernels, enter_project(): pl.pallas_call(functools.partial(enter_project_kernel, sizes, count), in_...  40.6 us
    pallas_call x1, Pallas kernels, widen(): pl.pallas_call(functools.partial(widen_kernel, count), in_specs=[ANY] * c...  5.45 us

profile of v3, /device:TPU:0, one launch (start us, length us, event | category | flops | bytes accessed | tf_op | source)
XLA Modules:
  0.0 242.1 jit_solution(9573430383166214197)
XLA Ops:
  0.6 0.7 stack.10
  1.3 0.7 stack.9
  2.0 0.5 dynamic_update_slice.3.refs_0_
  2.5 0.0 copy-start
  2.5 0.6 copy-done
  3.1 40.6 %shard_map.152 = (bf16[4,256,768]{2,1,0:T(8,128)(2,1)}, bf16[4,256,768]{2,1,0:T(8,128)(2,1)}, bf16[4,256,2304]{2,1,0:T(8,128)(2,1)}, f32[1024,128]{1,0:T(8,128)}...) custom-call(bf16[4,256,768]{2,1,0:T(8,128)(2,1)} %bitcast.15, ...), custom_call_target="tpu_custom_call" | custom-call | tf_op jit(solution)/shard_map/pallas_call | solution.py:1076
  43.7 52.3 %shard_map.153 = (bf16[1024,768]{1,0:T(8,128)(2,1)}, bf16[12,1024,1024]{2,1,0:T(8,128)(2,1)}, f32[1024,768]{1,0:T(8,128)}, f32[1024,768]{1,0:T(8,128)}, bf16[102...) custom-call(bf16[1024,2304]{1,0:T(8,128)(2,1)} %bitcast.18, ...), custom_call_target="tpu_custom_call" | custom-call | flops 12884901888 | bytes 10485760 | tf_op jit(solution)/shard_map/pallas_call | solution.py:1276
  96.0 71.1 %shard_map.154 = (f32[1024,768]{1,0:T(8,128)}, f32[1,768]{1,0:T(1,128)}, bf16[1024,768]{1,0:T(8,128)(2,1)}, bf16[1024,768]{1,0:T(8,128)(2,1)}, bf16[1024,768]{1,...) custom-call(f32[1024,768]{1,0:T(8,128)} %get-tuple-element.57.x1_ref, ...), custom_call_target="tpu_custom_call" | custom-call | flops 25769803776 | bytes 10485760 | tf_op jit(solution)/shard_map/pallas_call | solution.py:1299
  167.1 68.0 %shard_map.155 = (bf16[4,256,768]{2,1,0:T(8,128)(2,1)}, bf16[192,2304]{1,0:T(8,128)(2,1)}, bf16[192,768]{1,0:T(8,128)(2,1)}, bf16[192,2304]{1,0:T(8,128)(2,1)}, f32[8,768]{1,0:T(8,128)}) custom-call(f32[2,768]{1,0:T(2,128)} %get-tuple-element.51.gain_ref, f32[1,768]{1,0:T(1,128)} %get-tuple-element.71.other_gain_ref, ...), custom_call_target="tpu_custom_call" | custom-call | tf_op jit(solution)/shard_map/pallas_call | solution.py:1325
  235.2 5.5 %shard_map.156 = (f32[4,256,768]{2,1,0:T(8,128)}, f32[192,2304]{1,0:T(8,128)}, f32[192,2304]{1,0:T(8,128)}, f32[288,768]{1,0:T(8,128)}, f32[192,768]{1,0:T(8,128)}, /*index=5*/bf16[4,256,768]{2,1,0:T(8,128)(2,1)}) custom-call(bf16[4,256,768]{2,1,0:T(8,128)(2,1)} %get-tuple-element.81.refs_0_, bf16[192,2304]{1,0:T(8,128)(2,1)} %get-tuple-element.82.refs_1_, ...), custom_call_target="tpu_custom_call" | custom-call | tf_op jit(solution)/shard_map/pallas_call | solution.py:626
  240.6 1.4 fusion
  (2 shorter events, 0.0 us)
Async XLA Ops:
  2.5 0.6 copy-start
